TPU v7x, 32 devices: a whole 2x2x4 slice. The times are simulated.
32 devices in a mesh: geom: 2 (over x), aux: 16 (over z, y, core).
Axes of the slice: x: 2, y: 2, z: 4, core: 2. Of those that a mesh axis runs over, the one named last changes fastest.
Arguments:
- trial_vecs: float32 [8, 128, 224], P('geom', 'aux'), parts along dimension 0, may hold values from -6 to 6
- occ_energy: float32 [256], P('geom'), parts along dimension 0, may hold values from -1.5 to -0.2
- vir_energy: float32 [448], P('geom'), parts along dimension 0, may hold values from 0.2 to 2.5
- coul_ov: bfloat16 [2048, 128, 224], P(('geom', 'aux')), parts along dimension 0, may hold values from -0.03125 to 0.03125
- exch_oo: bfloat16 [2048, 128, 128], P(('geom', 'aux')), parts along dimension 0, may hold values from -0.0234375 to 0.0234375
- exch_vv: bfloat16 [2048, 224, 224], P(('geom', 'aux')), parts along dimension 0, may hold values from -0.375 to 0.375
Outputs:
- sigma_vecs: float32 [8, 128, 224], P('geom', 'aux'), parts along dimension 0
- update_vecs: float32 [8, 128, 224], P('geom', 'aux'), parts along dimension 0
There are 2 independent parts, one for each index of `geom`. A program takes and returns all parts, laid end to end along the dimension named above; each array names one. Nothing has to cross between parts.
All inputs are finite; a program needn't handle non-finite values.
Results may differ from a plain program's by a relative error of at most 0.0037.
Values may be sent and summed in bfloat16 or wider, within the bound.
No kernel may reach another device: no remote copies, remote signals or barrier semaphores. Data moves between devices by JAX's collectives and lax.ppermute only.
A program may use at most 64 MiB of HBM per device.

v0:
```python
import math
import jax
import jax.numpy as jnp
from jax import lax
from jax.sharding import PartitionSpec as P


def contract(totals, rows_x, coul_ov, exch_oo, exch_vv):
    aux_coef, exchange = totals
    height = rows_x.shape[1]
    n_occ = exch_oo.shape[1]
    n_virt = exch_vv.shape[1]
    aux_coef = jnp.einsum("pia,nia->np", coul_ov, rows_x, preferred_element_type=jnp.float32)
    aux_local = exch_vv.shape[0]
    group_size = math.gcd(aux_local, 16)
    group_count = aux_local // group_size
    vv_groups = exch_vv.reshape(group_count, group_size, n_virt, n_virt)
    oo_groups = exch_oo.reshape(group_count, group_size, n_occ, height)

    def advance(running, parts_pair):
        vv_part, oo_part = parts_pair
        halfway = jnp.einsum(
            "pab,njb->pnja", vv_part, rows_x, preferred_element_type=jnp.float32
        ).astype(jnp.bfloat16)
        return (
            running
            + jnp.einsum("pij,pnja->nia", oo_part, halfway, preferred_element_type=jnp.float32),
            None,
        )

    exchange, _ = lax.scan(advance, exchange, (vv_groups, oo_groups))
    return (aux_coef, exchange)


def residual_step(sigma_part, trial_part, diagonal, omega):
    resid = sigma_part - omega[:, None, None] * trial_part
    gap = jnp.maximum(jnp.abs(diagonal[None] - omega[:, None, None]), 1.0)
    return resid / gap


def on_device(trial_vecs, occ_energy, vir_energy, coul_ov, exch_oo, exch_vv):
    n_trial = trial_vecs.shape[0]
    local_rows = trial_vecs.shape[1]
    n_virt = trial_vecs.shape[2]
    n_occ = exch_oo.shape[1]
    aux_local = coul_ov.shape[0]
    empty = (
        jnp.zeros((n_trial, aux_local), jnp.float32),
        jnp.zeros((n_trial, n_occ, n_virt), jnp.float32),
    )
    row_start = lax.axis_index("aux") * local_rows
    wide_x = lax.all_gather(trial_vecs, "aux", axis=1, tiled=True)
    aux_coef, exchange = contract(empty, wide_x.astype(jnp.bfloat16), coul_ov, exch_oo, exch_vv)
    coulomb = jnp.einsum(
        "pia,np->nia", coul_ov, aux_coef.astype(jnp.bfloat16), preferred_element_type=jnp.float32
    )
    summed = lax.psum(2.0 * coulomb - exchange, "aux")
    diagonal = vir_energy[None, :] - occ_energy[:, None]
    sigma_all = diagonal[None] * wide_x + summed
    omega = jnp.sum(wide_x * sigma_all, axis=(1, 2)) / (
        jnp.sum(wide_x * wide_x, axis=(1, 2)) + 1e-06
    )
    precond = residual_step(sigma_all, wide_x, diagonal, omega)
    update_all = (
        precond * lax.rsqrt(jnp.mean(precond * precond, axis=(1, 2)) + 1e-06)[:, None, None]
    )
    sigma_vecs = lax.dynamic_slice_in_dim(sigma_all, row_start, local_rows, 1)
    update_vecs = lax.dynamic_slice_in_dim(update_all, row_start, local_rows, 1)
    return (sigma_vecs, update_vecs)


def solution(mesh):
    in_specs = (
        P("geom", "aux", None),
        P("geom"),
        P("geom"),
        P(("geom", "aux"), None, None),
        P(("geom", "aux"), None, None),
        P(("geom", "aux"), None, None),
    )
    out_specs = (P("geom", "aux", None), P("geom", "aux", None))
    return jax.shard_map(
        on_device, mesh=mesh, in_specs=in_specs, out_specs=out_specs, check_vma=False
    )
```

profile of v0, /device:TPU:0, one launch (start us, length us, event | category | flops | bytes accessed | tf_op | source)
XLA Modules:
  0.0 160.3 jit_solution(4688570363606826687)
XLA Ops:
  7.2 0.0 all-reduce.2.cloned.1.call-start
  7.2 0.8 copy.23
  8.0 24.6 %all_gather.3 = f32[4,128,224]{2,0,1:T(4,128)S(1)} all-gather(f32[4,8,224]{2,0,1:T(4,128)S(1)} %copy.23), channel_id=1, replica_groups=mesh['geom'=2,'aux'=16] {'aux'}, dimensions={1}, use_global_device_ids=true | all-gather | bytes 487424 | tf_op jit(solution)/shard_map/all_gather | solution.py:52
  32.6 0.4 multiply_reduce_fusion
  33.0 6.8 %copy.25 = bf16[64,128,224]{2,0,1:T(8,128)(2,1)} copy(bf16[64,128,224]{1,2,0:T(8,128)(2,1)} %param.11) | data formatting | bytes 7340032 | tf_op args[3]
  39.8 0.2 copy.28
  40.0 6.1 %fusion.25 = f32[4,128,224]{1,0,2:T(4,128)S(1)} fusion(bf16[64,128,224]{1,2,0:T(8,128)(2,1)} %param.11, bf16[4,128,224]{2,0,1:T(4,128)(2,1)S(1)} %get-tuple-element.84, bf16[64,128,224]{2,0,1:T(8,128)(2,1)} %copy.25), kind=kOutput, calls=%fused_computation.12 | convolution fusion | flops 29360384 | bytes 8028160 | tf_op jit(solution)/shard_map/pia,np->nia/dot_general | solution.py:54
  46.1 0.0 copy-start
  46.1 0.0 copy-start.1
  46.1 15.2 %while.11 = (s32[]{:T(128)}, f32[4,128,224]{1,2,0:T(8,128)S(1)}, bf16[4,16,224,224]{3,2,1,0:T(8,128)(2,1)}, bf16[4,128,224]{1,2,0:T(8,128)(2,1)S(1)}, bf16[4,16,...) while((s32[]{:T(128)}, f32[4,128,224]{1,2,0:T(8,128)S(1)}, ...), condition=%wide.region_1.2_spmd.clone, body=%wide.region_0.1_spmd.clone.sunk | while | flops 1293910016 | bytes 3507287 | solution.py:31
  46.1 3.8 %fusion.41 = f32[4,128,224]{1,2,0:T(8,128)S(1)} fusion(bf16[4,16,224,224]{3,2,1,0:T(8,128)(2,1)} %get-tuple-element.134, s32[]{:T(128)} %get-tuple-element.125, bf16[4,16,128,128]{3,2,1,0:T(8,128)(2,1)} %get-tuple-element.136, f32[4,128,224]{1,2,0:T(8,128)S(1)} %get-tuple-element.126, bf16[4,128,224]{1,2,0:T(8,128)(2,1)S(1)} %get-tuple-element.135, ...), kind=kOutput, calls=%fused_computation.7.clone.1 | convolution fusion | flops 1293910016 | bytes 3507201 | tf_op jit(solution)/shard_map/while/body/eval_jaxpr/pij,pnja->nia/dot_general | solution.py:27
  49.9 3.8 %fusion.41 = f32[4,128,224]{1,2,0:T(8,128)S(1)} fusion(bf16[4,16,224,224]{3,2,1,0:T(8,128)(2,1)} %get-tuple-element.134, s32[]{:T(128)} %get-tuple-element.125, bf16[4,16,128,128]{3,2,1,0:T(8,128)(2,1)} %get-tuple-element.136, f32[4,128,224]{1,2,0:T(8,128)S(1)} %get-tuple-element.126, bf16[4,128,224]{1,2,0:T(8,128)(2,1)S(1)} %get-tuple-element.135, ...), kind=kOutput, calls=%fused_computation.7.clone.1 | convolution fusion | flops 1293910016 | bytes 3507201 | tf_op jit(solution)/shard_map/while/body/eval_jaxpr/pij,pnja->nia/dot_general | solution.py:27
  53.7 3.8 %fusion.41 = f32[4,128,224]{1,2,0:T(8,128)S(1)} fusion(bf16[4,16,224,224]{3,2,1,0:T(8,128)(2,1)} %get-tuple-element.134, s32[]{:T(128)} %get-tuple-element.125, bf16[4,16,128,128]{3,2,1,0:T(8,128)(2,1)} %get-tuple-element.136, f32[4,128,224]{1,2,0:T(8,128)S(1)} %get-tuple-element.126, bf16[4,128,224]{1,2,0:T(8,128)(2,1)S(1)} %get-tuple-element.135, ...), kind=kOutput, calls=%fused_computation.7.clone.1 | convolution fusion | flops 1293910016 | bytes 3507201 | tf_op jit(solution)/shard_map/while/body/eval_jaxpr/pij,pnja->nia/dot_general | solution.py:27
  57.5 3.8 %fusion.41 = f32[4,128,224]{1,2,0:T(8,128)S(1)} fusion(bf16[4,16,224,224]{3,2,1,0:T(8,128)(2,1)} %get-tuple-element.134, s32[]{:T(128)} %get-tuple-element.125, bf16[4,16,128,128]{3,2,1,0:T(8,128)(2,1)} %get-tuple-element.136, f32[4,128,224]{1,2,0:T(8,128)S(1)} %get-tuple-element.126, bf16[4,128,224]{1,2,0:T(8,128)(2,1)S(1)} %get-tuple-element.135, ...), kind=kOutput, calls=%fused_computation.7.clone.1 | convolution fusion | flops 1293910016 | bytes 3507201 | tf_op jit(solution)/shard_map/while/body/eval_jaxpr/pij,pnja->nia/dot_general | solution.py:27
  61.3 0.8 fusion.29
  62.1 0.0 all-reduce.2.cloned.1.call-update
  62.2 0.2 copy.24
  62.4 0.0 copy-done
  62.4 0.0 copy-done.1
  62.4 0.1 broadcast_subtract_fusion
  62.5 87.5 %all-reduce.2.cloned.1.call-done = f32[4,128,224]{1,2,0:T(8,128)} async-done(((f32[4,128,224]{1,2,0:T(8,128)}), f32[4,128,224]{1,2,0:T(8,128)}) %all-reduce.2.cloned.1.call-update) | async-done | bytes 458768 | tf_op jit(solution)/shard_map/psum | solution.py:57
  150.1 1.2 multiply_reduce_fusion.2
  151.3 0.3 multiply_reduce_fusion.1
  151.6 0.3 dynamic-slice_multiply_fusion
  151.9 0.8 copy.31
  152.7 0.8 copy.32
  (3 shorter events, 0.0 us)
Async XLA Ops:
  7.2 142.9 %all-reduce.2.cloned.1.call-start = ((), (), s32[]{:S(2)}) async-start(), calls=%async_computation | async-start | bytes 917504 | tf_op jit(solution)/shard_map/psum | solution.py:57
  46.1 16.3 %copy-start = (f32[224]{0:T(256)S(1)}, f32[224]{0:T(256)}, u32[]{:S(2)}) copy-start(f32[224]{0:T(256)} %param.10) | copy-start | bytes 2692
  46.1 16.3 %copy-start.1 = (f32[128]{0:T(128)S(1)}, f32[128]{0:T(128)}, u32[]{:S(2)}) copy-start(f32[128]{0:T(128)} %param.9) | copy-start | bytes 1540
Sparse Core Ops, SparseCore 0:
  62.3 87.7 all-reduce.1
where the time goes:
time: 161 us; the launch traced here: 160 us
  waiting for transfers between devices  87.6 us (54%)
  blocking collectives  24.6 us (15%)
  matrix products  21.2 us (13%)
  between operations  14.1 us (9%)
  local copies, waits for them, and re-layouts  9.57 us (6%)
  other arithmetic  3.17 us (2%)
    psum x1, waiting for transfers between devices, on_device(): summed = lax.psum(2.0 * coulomb - exchange, 'aux')  87.5 us
    all_gather x1, blocking collectives, on_device(): wide_x = lax.all_gather(trial_vecs, 'aux', axis=1, tiled=True)  24.6 us
    dot_general x4, matrix products, advance(): jnp.einsum('pij,pnja->nia', oo_part, halfway, preferred_element_type=jnp....  15.1 us
    unnamed x9, local copies, waits for them, and re-layouts  9.34 us
    dot_general x1, matrix products, on_device(): jnp.einsum('pia,np->nia', coul_ov, aux_coef.astype(jnp.bfloat16), preferr...  6.1 us
  transfers between devices with their start and end apart: 1, of which 1 were waited for; matrix products, arithmetic and copies ran while one was open for 0% of the time, Pallas kernels for 0%

commit v1 on v0

--- a/solution.py
+++ b/solution.py
@@ -49,7 +49,16 @@
         jnp.zeros((n_trial, n_occ, n_virt), jnp.float32),
     )
     row_start = lax.axis_index("aux") * local_rows
-    wide_x = lax.all_gather(trial_vecs, "aux", axis=1, tiled=True)
+    ways = lax.axis_size("aux")
+    up = [(d, (d + 1) % ways) for d in range(ways)]
+    down = [(d, (d - 1) % ways) for d in range(ways)]
+    earlier, later = ([trial_vecs], [trial_vecs])
+    for __2 in range(ways // 2):
+        earlier.append(lax.ppermute(earlier[-1], "aux", up))
+    for __2 in range((ways - 1) // 2):
+        later.append(lax.ppermute(later[-1], "aux", down))
+    line = jnp.concatenate([*earlier[::-1], *later[1:]], axis=1)
+    wide_x = jnp.roll(line, (lax.axis_index("aux") - ways // 2) * trial_vecs.shape[1], axis=1)
     aux_coef, exchange = contract(empty, wide_x.astype(jnp.bfloat16), coul_ov, exch_oo, exch_vv)
     coulomb = jnp.einsum(
         "pia,np->nia", coul_ov, aux_coef.astype(jnp.bfloat16), preferred_element_type=jnp.float32

time: 161 us -> 251 us (1.56)
  starting transfers between devices: 0.04 us -> 55.7 us
  waiting for transfers between devices: 87.6 us -> 132 us
  blocking collectives: 24.6 us -> 0 us
  local copies, waits for them, and re-layouts: 9.57 us -> 20.2 us
  matrix products: 21.2 us -> 25.2 us
    ppermute x0 -> x15, starting transfers between devices: none -> 55.7 us  [the longest x8 46.2 us: on_device(): earlier.append(lax.ppermute(earlier[-1], 'aux', up))]
    ppermute x0 -> x15, waiting for transfers between devices: none -> 35.6 us  [the longest x8 35.6 us: on_device(): earlier.append(lax.ppermute(earlier[-1], 'aux', up))]
    all_gather x1 -> x0, blocking collectives: 24.6 us -> none  [on_device(): wide_x = lax.all_gather(trial_vecs, 'aux', axis=1, tiled=True)]
    concatenate x0 -> x1, local copies, waits for them, and re-layouts: none -> 17.2 us  [on_device(): jnp.roll(line, (lax.axis_index('aux') - ways // 2) * trial_vecs.shape[1],...]
    psum x1, waiting for transfers between devices: 87.5 us -> 96.4 us  [on_device(): summed = lax.psum(2.0 * coulomb - exchange, 'aux')]
    unnamed x9 -> x22, local copies, waits for them, and re-layouts: 9.34 us -> 2.77 us
    dot_general x4, matrix products: 15.1 us -> 18.3 us  [advance(): jnp.einsum('pij,pnja->nia', oo_part, halfway, preferred_element_type=jnp....]
  transfers between devices with their start and end apart: 1 -> 16, of which waited for: 1 -> 9; matrix products, arithmetic and copies ran while one was open for 0% -> 0% of each run, Pallas kernels for 0% -> 0%
where the time goes in v1:
time: 251 us; the launch traced here: 250 us
  waiting for transfers between devices  132 us (53%)
  starting transfers between devices  55.7 us (22%)
  matrix products  25.2 us (10%)
  local copies, waits for them, and re-layouts  20.2 us (8%)
  between operations  14.1 us (6%)
  other arithmetic  2.67 us (1%)
    psum x1, waiting for transfers between devices, on_device(): summed = lax.psum(2.0 * coulomb - exchange, 'aux')  96.4 us
    ppermute x8, starting transfers between devices, on_device(): earlier.append(lax.ppermute(earlier[-1], 'aux', up))  46.2 us
    ppermute x8, waiting for transfers between devices, on_device(): earlier.append(lax.ppermute(earlier[-1], 'aux', up))  35.6 us
    dot_general x4, matrix products, advance(): jnp.einsum('pij,pnja->nia', oo_part, halfway, preferred_element_type=jnp....  18.3 us
    concatenate x1, local copies, waits for them, and re-layouts, on_device(): jnp.roll(line, (lax.axis_index('aux') - ways // 2) * trial_vecs.shape[1],...  17.2 us
    ppermute x7, starting transfers between devices, on_device(): later.append(lax.ppermute(later[-1], 'aux', down))  9.48 us
    dot_general x1, matrix products, on_device(): jnp.einsum('pia,np->nia', coul_ov, aux_coef.astype(jnp.bfloat16), preferr...  6.88 us
  transfers between devices with their start and end apart: 16, of which 9 were waited for; matrix products, arithmetic and copies ran while one was open for 0% of the time, Pallas kernels for 0%

profile of v1, /device:TPU:0, one launch (start us, length us, event | category | flops | bytes accessed | tf_op | source)
XLA Modules:
  0.0 249.9 jit_solution(9001120703639517823)
XLA Ops:
  7.2 0.0 all-reduce.2.cloned.1.call-start
  7.2 1.0 copy.8
  8.2 0.5 collective-permute-start
  8.7 5.0 %collective-permute-start.8 = (f32[4,8,224]{1,0,2:T(4,128)S(1)}, f32[4,8,224]{1,0,2:T(4,128)S(1)}, u32[]{:S(2)}, u32[]{:S(2)}) collective-permute-start(f32[4,8,224]{1,0,2:T(4,128)S(1)} %copy.8), channel_id=1, source_target_pairs={{0,15},{1,0},{2,1},{3,2},{4,3},{5,4},{6,5},{7,6},{8,7},{9,8},{10,9... | collective-permute-start | bytes 86024 | tf_op jit(solution)/shard_map/ppermute | solution.py:59
  13.8 6.2 %collective-permute-done = f32[4,8,224]{1,0,2:T(4,128)S(1)} collective-permute-done((f32[4,8,224]{1,0,2:T(4,128)S(1)}, f32[4,8,224]{1,0,2:T(4,128)S(1)}, u32[]{:S(2)}, u32[]{:S(2)}) %collective-permute-start) | collective-permute-done | bytes 28704 | tf_op jit(solution)/shard_map/ppermute | solution.py:57
  20.0 1.7 collective-permute-start.1
  21.7 0.0 collective-permute-done.8
  21.7 2.8 %collective-permute-start.9 = (f32[4,8,224]{1,0,2:T(4,128)S(1)}, f32[4,8,224]{1,0,2:T(4,128)S(1)}, u32[]{:S(2)}, u32[]{:S(2)}) collective-permute-start(f32[4,8,224]{1,0,2:T(4,128)S(1)} %collective-permute-done.8), channel_id=1, source_target_pairs={{0,15},{1,0},{2,1},{3,2},{4,3},{5,4},{6,5},{7,6},{8,7},{9,8},{10,9... | collective-permute-start | bytes 86024 | tf_op jit(solution)/shard_map/ppermute | solution.py:59
  24.5 6.2 %collective-permute-done.1 = f32[4,8,224]{1,0,2:T(4,128)S(1)} collective-permute-done((f32[4,8,224]{1,0,2:T(4,128)S(1)}, f32[4,8,224]{1,0,2:T(4,128)S(1)}, u32[]{:S(2)}, u32[]{:S(2)}) %collective-permute-start.1) | collective-permute-done | bytes 28704 | tf_op jit(solution)/shard_map/ppermute | solution.py:57
  30.7 3.1 %collective-permute-start.2 = (f32[4,8,224]{1,0,2:T(4,128)S(1)}, f32[4,8,224]{1,0,2:T(4,128)S(1)}, u32[]{:S(2)}, u32[]{:S(2)}) collective-permute-start(f32[4,8,224]{1,0,2:T(4,128)S(1)} %collective-permute-done.1), channel_id=1, source_target_pairs={{0,1},{1,2},{2,3},{3,4},{4,5},{5,6},{6,7},{7,8},{8,9},{9,10},{10,1... | collective-permute-start | bytes 86024 | tf_op jit(solution)/shard_map/ppermute | solution.py:57
  33.7 0.0 collective-permute-done.9
  33.7 1.4 collective-permute-start.10
  35.2 6.2 %collective-permute-done.2 = f32[4,8,224]{1,0,2:T(4,128)S(1)} collective-permute-done((f32[4,8,224]{1,0,2:T(4,128)S(1)}, f32[4,8,224]{1,0,2:T(4,128)S(1)}, u32[]{:S(2)}, u32[]{:S(2)}) %collective-permute-start.2) | collective-permute-done | bytes 28704 | tf_op jit(solution)/shard_map/ppermute | solution.py:57
  41.4 0.0 copy-start
  41.4 4.4 %collective-permute-start.3 = (f32[4,8,224]{1,0,2:T(4,128)S(1)}, f32[4,8,224]{1,0,2:T(4,128)S(1)}, u32[]{:S(2)}, u32[]{:S(2)}) collective-permute-start(f32[4,8,224]{1,0,2:T(4,128)S(1)} %collective-permute-done.2), channel_id=1, source_target_pairs={{0,1},{1,2},{2,3},{3,4},{4,5},{5,6},{6,7},{7,8},{8,9},{9,10},{10,1... | collective-permute-start | bytes 86024 | tf_op jit(solution)/shard_map/ppermute | solution.py:57
  45.8 0.0 collective-permute-done.10
  45.8 0.0 copy-start.1
  45.8 0.1 collective-permute-start.11
  45.9 6.1 %collective-permute-done.3 = f32[4,8,224]{1,0,2:T(4,128)S(1)} collective-permute-done((f32[4,8,224]{1,0,2:T(4,128)S(1)}, f32[4,8,224]{1,0,2:T(4,128)S(1)}, u32[]{:S(2)}, u32[]{:S(2)}) %collective-permute-start.3) | collective-permute-done | bytes 28704 | tf_op jit(solution)/shard_map/ppermute | solution.py:57
  52.0 6.6 %collective-permute-start.4 = (f32[4,8,224]{1,0,2:T(4,128)S(1)}, f32[4,8,224]{1,0,2:T(4,128)S(1)}, u32[]{:S(2)}, u32[]{:S(2)}) collective-permute-start(f32[4,8,224]{1,0,2:T(4,128)S(1)} %collective-permute-done.3), channel_id=1, source_target_pairs={{0,1},{1,2},{2,3},{3,4},{4,5},{5,6},{6,7},{7,8},{8,9},{9,10},{10,1... | collective-permute-start | bytes 86024 | tf_op jit(solution)/shard_map/ppermute | solution.py:57
  58.6 0.0 collective-permute-done.11
  58.6 0.0 copy-done.2
  58.6 0.0 copy-start.3
  58.6 0.1 collective-permute-start.12
  58.7 4.0 %collective-permute-done.4 = f32[4,8,224]{1,0,2:T(4,128)S(1)} collective-permute-done((f32[4,8,224]{1,0,2:T(4,128)S(1)}, f32[4,8,224]{1,0,2:T(4,128)S(1)}, u32[]{:S(2)}, u32[]{:S(2)}) %collective-permute-start.4) | collective-permute-done | bytes 28704 | tf_op jit(solution)/shard_map/ppermute | solution.py:57
  62.6 0.0 copy-done.3
  62.6 0.0 copy-start.4
  62.6 8.8 %collective-permute-start.5 = (f32[4,8,224]{1,0,2:T(4,128)S(1)}, f32[4,8,224]{1,0,2:T(4,128)S(1)}, u32[]{:S(2)}, u32[]{:S(2)}) collective-permute-start(f32[4,8,224]{1,0,2:T(4,128)S(1)} %collective-permute-done.4), channel_id=1, source_target_pairs={{0,1},{1,2},{2,3},{3,4},{4,5},{5,6},{6,7},{7,8},{8,9},{9,10},{10,1... | collective-permute-start | bytes 86024 | tf_op jit(solution)/shard_map/ppermute | solution.py:57
  71.4 0.0 collective-permute-done.12
  71.4 0.0 copy-done.4
  71.4 0.0 copy-start.5
  71.4 0.1 collective-permute-start.13
  71.5 2.1 collective-permute-done.5
  73.6 0.0 copy-done.5
  73.6 0.0 copy-start.6
  73.6 10.6 %collective-permute-start.6 = (f32[4,8,224]{1,0,2:T(4,128)S(1)}, f32[4,8,224]{1,0,2:T(4,128)}, u32[]{:S(2)}, u32[]{:S(2)}) collective-permute-start(f32[4,8,224]{1,0,2:T(4,128)S(1)} %collective-permute-done.5), channel_id=1, source_target_pairs={{0,1},{1,2},{2,3},{3,4},{4,5},{5,6},{6,7},{7,8},{8,9},{9,10},{10,1... | collective-permute-start | bytes 86024 | tf_op jit(solution)/shard_map/ppermute | solution.py:57
  84.3 0.0 collective-permute-done.13
  84.3 0.0 copy-done.6
  84.3 0.0 collective-permute-start.14
  84.3 2.3 collective-permute-done.6
  86.6 10.5 %collective-permute-start.7 = (f32[4,8,224]{1,0,2:T(4,128)}, f32[4,8,224]{1,0,2:T(4,128)}, u32[]{:S(2)}, u32[]{:S(2)}) collective-permute-start(f32[4,8,224]{1,0,2:T(4,128)} %collective-permute-done.6), channel_id=1, source_target_pairs={{0,1},{1,2},{2,3},{3,4},{4,5},{5,6},{6,7},{7,8},{8,9},{9,10},{10,1... | collective-permute-start | bytes 86024 | tf_op jit(solution)/shard_map/ppermute | solution.py:57
  97.1 0.0 collective-permute-done.14
  97.1 0.0 copy-done
  97.1 0.0 copy-done.1
  97.1 2.5 collective-permute-done.7
  99.5 17.2 %concatenate.6 = f32[4,256,224]{1,0,2:T(4,128)S(1)} concatenate(f32[4,8,224]{1,0,2:T(4,128)} %collective-permute-done.7, f32[4,8,224]{1,0,2:T(4,128)} %collective-permute-done.6, f32[4,8,224]{1,0,2:T(4,128)} %copy-done.6, f32[4,8,224]{1,0,2:T(4,128)} %copy-done.4, f32[4,8,224]{1,0,2:T(4,128)} %copy-done.2, f32[4,8,224]{1,0,2:T(4,128)} %copy-done, ...), dimensions={1} | concatenate | bytes 1835008 | tf_op jit(solution)/shard_map/jit(_roll_dynamic)/concatenate | solution.py:61
  116.8 0.2 dynamic-slice_convert_fusion
  117.0 0.2 copy.13
  117.2 18.3 %while.11 = (s32[]{:T(128)}, f32[4,128,224]{1,2,0:T(8,128)}, bf16[4,16,224,224]{3,2,1,0:T(8,128)(2,1)}, bf16[4,128,224]{2,1,0:T(8,128)(2,1)S(1)}, bf16[4,16,128,128]{3,2,1,0:T(8,128)(2,1)}, /*index=5*/s32[]{:T(128)}, s32[]{:T(128)}) while((s32[]{:T(128)}, f32[4,128,224]{1,2,0:T(8,128)}, bf16[4,16,224,224]{3,2,1,0:T(8,128)(2,1)}, ...), condition=%wide.region_1.2_spmd.clone, body=%wide.region_0.1_spmd.clone.sunk | while | flops 1293910016 | bytes 3507287 | solution.py:31
  117.2 4.5 %fusion.56 = f32[4,128,224]{1,2,0:T(8,128)} fusion(bf16[4,16,224,224]{3,2,1,0:T(8,128)(2,1)} %get-tuple-element.119, s32[]{:T(128)} %get-tuple-element.110, bf16[4,16,128,128]{3,2,1,0:T(8,128)(2,1)} %get-tuple-element.121, f32[4,128,224]{1,2,0:T(8,128)} %get-tuple-element.111, bf16[4,128,224]{2,1,0:T(8,128)(2,1)S(1)} %get-tuple-element.120, ...), kind=kOutput, calls=%fused_computation.7.clone.1 | convolution fusion | flops 1293910016 | bytes 3507201 | tf_op jit(solution)/shard_map/while/body/eval_jaxpr/pij,pnja->nia/dot_general | solution.py:27
  121.6 4.6 %fusion.56 = f32[4,128,224]{1,2,0:T(8,128)} fusion(bf16[4,16,224,224]{3,2,1,0:T(8,128)(2,1)} %get-tuple-element.119, s32[]{:T(128)} %get-tuple-element.110, bf16[4,16,128,128]{3,2,1,0:T(8,128)(2,1)} %get-tuple-element.121, f32[4,128,224]{1,2,0:T(8,128)} %get-tuple-element.111, bf16[4,128,224]{2,1,0:T(8,128)(2,1)S(1)} %get-tuple-element.120, ...), kind=kOutput, calls=%fused_computation.7.clone.1 | convolution fusion | flops 1293910016 | bytes 3507201 | tf_op jit(solution)/shard_map/while/body/eval_jaxpr/pij,pnja->nia/dot_general | solution.py:27
  126.3 4.6 %fusion.56 = f32[4,128,224]{1,2,0:T(8,128)} fusion(bf16[4,16,224,224]{3,2,1,0:T(8,128)(2,1)} %get-tuple-element.119, s32[]{:T(128)} %get-tuple-element.110, bf16[4,16,128,128]{3,2,1,0:T(8,128)(2,1)} %get-tuple-element.121, f32[4,128,224]{1,2,0:T(8,128)} %get-tuple-element.111, bf16[4,128,224]{2,1,0:T(8,128)(2,1)S(1)} %get-tuple-element.120, ...), kind=kOutput, calls=%fused_computation.7.clone.1 | convolution fusion | flops 1293910016 | bytes 3507201 | tf_op jit(solution)/shard_map/while/body/eval_jaxpr/pij,pnja->nia/dot_general | solution.py:27
  130.9 4.6 %fusion.56 = f32[4,128,224]{1,2,0:T(8,128)} fusion(bf16[4,16,224,224]{3,2,1,0:T(8,128)(2,1)} %get-tuple-element.119, s32[]{:T(128)} %get-tuple-element.110, bf16[4,16,128,128]{3,2,1,0:T(8,128)(2,1)} %get-tuple-element.121, f32[4,128,224]{1,2,0:T(8,128)} %get-tuple-element.111, bf16[4,128,224]{2,1,0:T(8,128)(2,1)S(1)} %get-tuple-element.120, ...), kind=kOutput, calls=%fused_computation.7.clone.1 | convolution fusion | flops 1293910016 | bytes 3507201 | tf_op jit(solution)/shard_map/while/body/eval_jaxpr/pij,pnja->nia/dot_general | solution.py:27
  135.5 6.9 %fusion.32 = f32[4,128,224]{1,0,2:T(4,128)} fusion(bf16[64,128,224]{1,2,0:T(8,128)(2,1)} %param.11, bf16[4,128,224]{1,0,2:T(4,128)(2,1)S(1)} %dynamic-slice_convert_fusion, f32[4,128,224]{1,2,0:T(8,128)} %get-tuple-element.29), kind=kOutput, calls=%fused_computation.17 | convolution fusion | flops 29589760 | bytes 4816896 | tf_op jit(solution)/shard_map/pia,np->nia/dot_general | solution.py:63
  142.4 0.0 all-reduce.2.cloned.1.call-update
  142.4 0.0 copy-done.7
  142.4 0.0 copy-done.8
  142.4 0.1 broadcast_subtract_fusion
  142.5 96.4 %all-reduce.2.cloned.1.call-done = f32[4,128,224]{1,0,2:T(4,128)} async-done(((f32[4,128,224]{1,0,2:T(4,128)}), f32[4,128,224]{1,0,2:T(4,128)}) %all-reduce.2.cloned.1.call-update) | async-done | bytes 458768 | tf_op jit(solution)/shard_map/psum | solution.py:66
  238.9 1.5 multiply_reduce_fusion.1
  240.4 0.5 multiply_reduce_fusion
  240.9 0.6 dynamic-slice_multiply_fusion
  241.5 0.8 copy.15
  242.3 0.8 copy.16
  (6 shorter events, 0.0 us)
Async XLA Ops:
  7.2 231.7 %all-reduce.2.cloned.1.call-start = ((), (), s32[]{:S(2)}) async-start(), calls=%async_computation | async-start | bytes 917504 | tf_op jit(solution)/shard_map/psum | solution.py:66
  8.2 11.8 %collective-permute-start = (f32[4,8,224]{1,0,2:T(4,128)S(1)}, f32[4,8,224]{1,0,2:T(4,128)S(1)}, u32[]{:S(2)}, u32[]{:S(2)}) collective-permute-start(f32[4,8,224]{1,0,2:T(4,128)S(1)} %copy.8), channel_id=1, source_target_pairs={{0,1},{1,2},{2,3},{3,4},{4,5},{5,6},{6,7},{7,8},{8,9},{9,10},{10,1... | collective-permute-start | bytes 86024 | tf_op jit(solution)/shard_map/ppermute | solution.py:57
  8.7 13.0 %collective-permute-start.8 = (f32[4,8,224]{1,0,2:T(4,128)S(1)}, f32[4,8,224]{1,0,2:T(4,128)S(1)}, u32[]{:S(2)}, u32[]{:S(2)}) collective-permute-start(f32[4,8,224]{1,0,2:T(4,128)S(1)} %copy.8), channel_id=1, source_target_pairs={{0,15},{1,0},{2,1},{3,2},{4,3},{5,4},{6,5},{7,6},{8,7},{9,8},{10,9... | collective-permute-start | bytes 86024 | tf_op jit(solution)/shard_map/ppermute | solution.py:59
  20.0 10.7 %collective-permute-start.1 = (f32[4,8,224]{1,0,2:T(4,128)S(1)}, f32[4,8,224]{1,0,2:T(4,128)S(1)}, u32[]{:S(2)}, u32[]{:S(2)}) collective-permute-start(f32[4,8,224]{1,0,2:T(4,128)S(1)} %collective-permute-done), channel_id=1, source_target_pairs={{0,1},{1,2},{2,3},{3,4},{4,5},{5,6},{6,7},{7,8},{8,9},{9,10},{10,1... | collective-permute-start | bytes 86024 | tf_op jit(solution)/shard_map/ppermute | solution.py:57
  21.7 12.0 %collective-permute-start.9 = (f32[4,8,224]{1,0,2:T(4,128)S(1)}, f32[4,8,224]{1,0,2:T(4,128)S(1)}, u32[]{:S(2)}, u32[]{:S(2)}) collective-permute-start(f32[4,8,224]{1,0,2:T(4,128)S(1)} %collective-permute-done.8), channel_id=1, source_target_pairs={{0,15},{1,0},{2,1},{3,2},{4,3},{5,4},{6,5},{7,6},{8,7},{9,8},{10,9... | collective-permute-start | bytes 86024 | tf_op jit(solution)/shard_map/ppermute | solution.py:59
  30.7 10.7 %collective-permute-start.2 = (f32[4,8,224]{1,0,2:T(4,128)S(1)}, f32[4,8,224]{1,0,2:T(4,128)S(1)}, u32[]{:S(2)}, u32[]{:S(2)}) collective-permute-start(f32[4,8,224]{1,0,2:T(4,128)S(1)} %collective-permute-done.1), channel_id=1, source_target_pairs={{0,1},{1,2},{2,3},{3,4},{4,5},{5,6},{6,7},{7,8},{8,9},{9,10},{10,1... | collective-permute-start | bytes 86024 | tf_op jit(solution)/shard_map/ppermute | solution.py:57
  33.7 12.1 %collective-permute-start.10 = (f32[4,8,224]{1,0,2:T(4,128)S(1)}, f32[4,8,224]{1,0,2:T(4,128)S(1)}, u32[]{:S(2)}, u32[]{:S(2)}) collective-permute-start(f32[4,8,224]{1,0,2:T(4,128)S(1)} %collective-permute-done.9), channel_id=1, source_target_pairs={{0,15},{1,0},{2,1},{3,2},{4,3},{5,4},{6,5},{7,6},{8,7},{9,8},{10,9... | collective-permute-start | bytes 86024 | tf_op jit(solution)/shard_map/ppermute | solution.py:59
  41.4 55.7 %copy-start = (f32[4,8,224]{1,0,2:T(4,128)}, f32[4,8,224]{1,0,2:T(4,128)S(1)}, u32[]{:S(2)}) copy-start(f32[4,8,224]{1,0,2:T(4,128)S(1)} %collective-permute-done.2) | copy-start | bytes 86020
  41.4 10.7 %collective-permute-start.3 = (f32[4,8,224]{1,0,2:T(4,128)S(1)}, f32[4,8,224]{1,0,2:T(4,128)S(1)}, u32[]{:S(2)}, u32[]{:S(2)}) collective-permute-start(f32[4,8,224]{1,0,2:T(4,128)S(1)} %collective-permute-done.2), channel_id=1, source_target_pairs={{0,1},{1,2},{2,3},{3,4},{4,5},{5,6},{6,7},{7,8},{8,9},{9,10},{10,1... | collective-permute-start | bytes 86024 | tf_op jit(solution)/shard_map/ppermute | solution.py:57
  45.8 51.3 %copy-start.1 = (f32[4,8,224]{1,0,2:T(4,128)}, f32[4,8,224]{1,0,2:T(4,128)S(1)}, u32[]{:S(2)}) copy-start(f32[4,8,224]{1,0,2:T(4,128)S(1)} %collective-permute-done.10) | copy-start | bytes 86020
  45.8 12.8 %collective-permute-start.11 = (f32[4,8,224]{1,0,2:T(4,128)S(1)}, f32[4,8,224]{1,0,2:T(4,128)S(1)}, u32[]{:S(2)}, u32[]{:S(2)}) collective-permute-start(f32[4,8,224]{1,0,2:T(4,128)S(1)} %collective-permute-done.10), channel_id=1, source_target_pairs={{0,15},{1,0},{2,1},{3,2},{4,3},{5,4},{6,5},{7,6},{8,7},{9,8},{10,9... | collective-permute-start | bytes 86024 | tf_op jit(solution)/shard_map/ppermute | solution.py:59
  52.0 6.6 %copy-start.2 = (f32[4,8,224]{1,0,2:T(4,128)}, f32[4,8,224]{1,0,2:T(4,128)S(1)}, u32[]{:S(2)}) copy-start(f32[4,8,224]{1,0,2:T(4,128)S(1)} %collective-permute-done.3) | copy-start | bytes 86020
  52.0 10.6 %collective-permute-start.4 = (f32[4,8,224]{1,0,2:T(4,128)S(1)}, f32[4,8,224]{1,0,2:T(4,128)S(1)}, u32[]{:S(2)}, u32[]{:S(2)}) collective-permute-start(f32[4,8,224]{1,0,2:T(4,128)S(1)} %collective-permute-done.3), channel_id=1, source_target_pairs={{0,1},{1,2},{2,3},{3,4},{4,5},{5,6},{6,7},{7,8},{8,9},{9,10},{10,1... | collective-permute-start | bytes 86024 | tf_op jit(solution)/shard_map/ppermute | solution.py:57
  58.6 4.0 %copy-start.3 = (f32[4,8,224]{1,0,2:T(4,128)}, f32[4,8,224]{1,0,2:T(4,128)S(1)}, u32[]{:S(2)}) copy-start(f32[4,8,224]{1,0,2:T(4,128)S(1)} %collective-permute-done.11) | copy-start | bytes 86020
  58.6 12.8 %collective-permute-start.12 = (f32[4,8,224]{1,0,2:T(4,128)S(1)}, f32[4,8,224]{1,0,2:T(4,128)S(1)}, u32[]{:S(2)}, u32[]{:S(2)}) collective-permute-start(f32[4,8,224]{1,0,2:T(4,128)S(1)} %collective-permute-done.11), channel_id=1, source_target_pairs={{0,15},{1,0},{2,1},{3,2},{4,3},{5,4},{6,5},{7,6},{8,7},{9,8},{10,9... | collective-permute-start | bytes 86024 | tf_op jit(solution)/shard_map/ppermute | solution.py:59
  62.6 8.8 %copy-start.4 = (f32[4,8,224]{1,0,2:T(4,128)}, f32[4,8,224]{1,0,2:T(4,128)S(1)}, u32[]{:S(2)}) copy-start(f32[4,8,224]{1,0,2:T(4,128)S(1)} %collective-permute-done.4) | copy-start | bytes 86020
  62.6 11.0 %collective-permute-start.5 = (f32[4,8,224]{1,0,2:T(4,128)S(1)}, f32[4,8,224]{1,0,2:T(4,128)S(1)}, u32[]{:S(2)}, u32[]{:S(2)}) collective-permute-start(f32[4,8,224]{1,0,2:T(4,128)S(1)} %collective-permute-done.4), channel_id=1, source_target_pairs={{0,1},{1,2},{2,3},{3,4},{4,5},{5,6},{6,7},{7,8},{8,9},{9,10},{10,1... | collective-permute-start | bytes 86024 | tf_op jit(solution)/shard_map/ppermute | solution.py:57
  71.4 2.2 copy-start.5
  71.4 12.8 %collective-permute-start.13 = (f32[4,8,224]{1,0,2:T(4,128)S(1)}, f32[4,8,224]{1,0,2:T(4,128)}, u32[]{:S(2)}, u32[]{:S(2)}) collective-permute-start(f32[4,8,224]{1,0,2:T(4,128)S(1)} %collective-permute-done.12), channel_id=1, source_target_pairs={{0,15},{1,0},{2,1},{3,2},{4,3},{5,4},{6,5},{7,6},{8,7},{9,8},{10,9... | collective-permute-start | bytes 86024 | tf_op jit(solution)/shard_map/ppermute | solution.py:59
  73.6 10.6 %copy-start.6 = (f32[4,8,224]{1,0,2:T(4,128)}, f32[4,8,224]{1,0,2:T(4,128)S(1)}, u32[]{:S(2)}) copy-start(f32[4,8,224]{1,0,2:T(4,128)S(1)} %collective-permute-done.5) | copy-start | bytes 86020
  73.6 12.9 %collective-permute-start.6 = (f32[4,8,224]{1,0,2:T(4,128)S(1)}, f32[4,8,224]{1,0,2:T(4,128)}, u32[]{:S(2)}, u32[]{:S(2)}) collective-permute-start(f32[4,8,224]{1,0,2:T(4,128)S(1)} %collective-permute-done.5), channel_id=1, source_target_pairs={{0,1},{1,2},{2,3},{3,4},{4,5},{5,6},{6,7},{7,8},{8,9},{9,10},{10,1... | collective-permute-start | bytes 86024 | tf_op jit(solution)/shard_map/ppermute | solution.py:57
  84.3 12.8 %collective-permute-start.14 = (f32[4,8,224]{1,0,2:T(4,128)}, f32[4,8,224]{1,0,2:T(4,128)}, u32[]{:S(2)}, u32[]{:S(2)}) collective-permute-start(f32[4,8,224]{1,0,2:T(4,128)} %collective-permute-done.13), channel_id=1, source_target_pairs={{0,15},{1,0},{2,1},{3,2},{4,3},{5,4},{6,5},{7,6},{8,7},{9,8},{10,9... | collective-permute-start | bytes 86024 | tf_op jit(solution)/shard_map/ppermute | solution.py:59
  86.6 13.0 %collective-permute-start.7 = (f32[4,8,224]{1,0,2:T(4,128)}, f32[4,8,224]{1,0,2:T(4,128)}, u32[]{:S(2)}, u32[]{:S(2)}) collective-permute-start(f32[4,8,224]{1,0,2:T(4,128)} %collective-permute-done.6), channel_id=1, source_target_pairs={{0,1},{1,2},{2,3},{3,4},{4,5},{5,6},{6,7},{7,8},{8,9},{9,10},{10,1... | collective-permute-start | bytes 86024 | tf_op jit(solution)/shard_map/ppermute | solution.py:57
  135.5 6.9 %copy-start.7 = (f32[224]{0:T(256)S(1)}, f32[224]{0:T(256)}, u32[]{:S(2)}) copy-start(f32[224]{0:T(256)} %param.10) | copy-start | bytes 2692
  135.5 6.9 %copy-start.8 = (f32[128]{0:T(128)S(1)}, f32[128]{0:T(128)}, u32[]{:S(2)}) copy-start(f32[128]{0:T(128)} %param.9) | copy-start | bytes 1540
Sparse Core Ops, SparseCore 0:
  142.5 96.3 all-reduce.1
